TPU v7x, 512 devices: a whole 4x4x16 slice. The times are simulated.
512 devices in a mesh: expert: 64 (over x, z), tensor: 8 (over y, core).
Axes of the slice: x: 4, y: 4, z: 16, core: 2. Of those that a mesh axis runs over, the one named last changes fastest.
Arguments:
- tokens: bfloat16 [1024, 7168], P('expert', 'tensor'), may hold values from -6 to 6
- expert_ids: int32 [1024, 8], P('expert'), may hold values from 0 to 31, as said below
- route_weights: float32 [1024, 8], P('expert'), may hold values from 0.05 to 1
- gate_weight: bfloat16 [64, 512, 7168], P('expert', 'tensor'), may hold values from -0.0625 to 0.0625
- up_weight: bfloat16 [64, 512, 7168], P('expert', 'tensor'), may hold values from -0.0625 to 0.0625
- down_weight: bfloat16 [64, 512, 7168], P('expert', 'tensor'), may hold values from -0.1875 to 0.1875
Outputs:
- mixed: bfloat16 [1024, 7168], P('expert', 'tensor')
Inputs may be any that keep to these rules, and one draw needn't show every extreme that they name: `expert_ids`: each row holds 8 different experts. One expert, the same for all tokens, is named by exactly 4 of the 16 tokens of every block of 16 consecutive tokens; every other expert by at most 4 tokens of a block.
All inputs are finite; a program needn't handle non-finite values.
Results may differ from a plain program's by a relative error of at most 0.015.
Values may be sent and summed in bfloat16 or wider, within the bound.
No kernel may reach another device: no remote copies, remote signals or barrier semaphores. Data moves between devices by JAX's collectives and lax.ppermute only.
A program may use at most 64 MiB of HBM per device.

v0:
```python
import jax
import jax.numpy as jnp
from jax import lax
from jax.sharding import PartitionSpec as P


def in_order(blocks, dim):
    shape = list(blocks.shape[1:])
    shape[dim] *= blocks.shape[0]
    return jnp.moveaxis(blocks, 0, dim).reshape(shape)


def sent_to_all(shard, axis):
    copies = jnp.broadcast_to(shard, (lax.axis_size(axis), *shard.shape))
    return lax.all_to_all(copies, axis, split_axis=0, concat_axis=0, tiled=True)


def gather_directly(shard, axis, dim):
    return in_order(sent_to_all(shard, axis), dim)


def rows_times(rows, weight):
    return lax.dot_general(
        rows, weight, (((1,), (1,)), ((), ())), preferred_element_type=jnp.float32
    )


def body(tokens, expert_ids, route_weights, gate_weight, up_weight, down_weight):
    devices_wide = lax.axis_size("expert")
    experts = devices_wide // 2
    tok_count = expert_ids.shape[0]
    per_token = expert_ids.shape[1]
    capacity = min(tok_count, tok_count * per_token // experts)
    slot_count = experts * capacity
    arrived_count = devices_wide * capacity
    expert_range = jnp.arange(experts, dtype=jnp.int32)
    onehot = jnp.sum(
        (expert_ids[:, :, None] == expert_range[None, None, :]).astype(jnp.int32), axis=1
    )
    earlier_count = jnp.cumsum(onehot, axis=0) - onehot
    slot_rank = jnp.take_along_axis(earlier_count, expert_ids, axis=1)
    slot_of = expert_ids * capacity + slot_rank
    slot_range = jnp.arange(slot_count, dtype=jnp.int32)
    select = jnp.any(slot_of[None, :, :] == slot_range[:, None, None], axis=2).astype(jnp.bfloat16)
    weight_gate = gate_weight[0]
    weight_up = up_weight[0]
    weight_out = down_weight[0]
    packed = jnp.dot(select, tokens, preferred_element_type=jnp.float32).astype(jnp.bfloat16)
    packed = packed.reshape(experts, capacity, tokens.shape[1])
    arrived = lax.all_to_all(
        jnp.repeat(packed, 2, axis=0), "expert", split_axis=0, concat_axis=0, tiled=True
    ).reshape(arrived_count, -1)
    shard_piece = lax.all_gather(arrived, "tensor", axis=1, tiled=True)
    gate_act = rows_times(shard_piece, weight_gate)
    up_act = rows_times(shard_piece, weight_up)
    hidden = (jax.nn.silu(gate_act) * up_act).astype(jnp.bfloat16)
    columns = lax.all_to_all(weight_out, "tensor", split_axis=1, concat_axis=0, tiled=True)
    unit_count = hidden.shape[1]
    shard_piece = gather_directly(hidden, "tensor", 1)
    groups = shard_piece.shape[1] // unit_count
    weight_rows = columns
    weight_rows = weight_rows.reshape(groups, unit_count, columns.shape[1])
    grouped = shard_piece.reshape(shard_piece.shape[0], groups, unit_count)
    group_terms = jnp.einsum(
        "rgf,gfd->grd", grouped, weight_rows, preferred_element_type=jnp.float32
    ).astype(jnp.bfloat16)
    group_terms = lax.optimization_barrier(group_terms)
    half_out = jnp.sum(group_terms.astype(jnp.float32), axis=0).astype(jnp.bfloat16)
    returned = lax.all_to_all(
        half_out.reshape(devices_wide, capacity, -1),
        "expert",
        split_axis=0,
        concat_axis=0,
        tiled=True,
    )
    returned = returned.reshape(experts, 2, capacity, -1).astype(jnp.float32)
    combined = (returned[:, 0] + returned[:, 1]).reshape(slot_count, -1)
    picked = combined[slot_of]
    mixed_out = jnp.sum(route_weights[:, :, None] * picked, axis=1)
    return mixed_out.astype(jnp.bfloat16)


def solution(mesh):
    placed = (
        P("expert", "tensor"),
        P("expert", None),
        P("expert", None),
        P("expert", "tensor", None),
        P("expert", "tensor", None),
        P("expert", "tensor", None),
    )
    return jax.shard_map(
        body, mesh=mesh, in_specs=placed, out_specs=P("expert", "tensor"), check_vma=False
    )
```

profile of v0, /device:TPU:6, one launch (start us, length us, event | category | flops | bytes accessed | tf_op | source)
XLA Modules:
  0.0 163.6 jit_solution(6472989712273088661)
XLA Ops:
  6.5 0.8 copy.21
  7.4 0.7 bitcast_or_fusion
  8.1 0.1 convert_reduce_fusion
  8.2 0.1 copy.22
  8.3 0.1 reshape.51
  8.4 1.3 gather_fusion.1
  9.7 0.1 reshape.54
  9.9 0.1 copy.24
  9.9 0.1 fusion.7
  10.1 0.3 convolution_convert_fusion.1
  10.4 0.1 broadcast_in_dim.19
  10.5 47.4 %all_to_all.31 = bf16[64,4,896]{2,1,0:T(4,128)(2,1)S(1)} all-to-all(bf16[64,4,896]{2,1,0:T(4,128)(2,1)S(1)} %bitcast.31), channel_id=1, replica_groups=mesh['expert'=64,'tensor'=8] {'expert'}, dimensions={0} | all-to-all | bytes 917504 | tf_op jit(solution)/shard_map/all_to_all | solution.py:50
  57.9 0.9 reshape.40
  58.8 0.1 copy.27
  59.0 1.1 copy.25
  60.0 4.6 %all-to-all-start.2 = ((bf16[64,8,896]{2,0,1:T(8,128)(2,1)}), bf16[64,8,896]{2,0,1:T(8,128)(2,1)S(1)}, u32[]{:S(2)}, u32[]{:S(2)}) async-start(bf16[64,8,896]{2,0,1:T(8,128)(2,1)} %copy.25), calls=%async_computation.2 | async-start | bytes 1835008 | tf_op jit(solution)/shard_map/all_to_all | solution.py:57
  64.7 30.6 %all-gather.2.cloned.1.call-done = bf16[256,7168]{1,0:T(8,128)(2,1)} async-done(((bf16[256,896]{1,0:T(8,128)(2,1)}), bf16[256,7168]{1,0:T(8,128)(2,1)}) %all-gather.2.cloned.1.call-update) | async-done | bytes 3670032 | tf_op jit(solution)/shard_map/all_gather | solution.py:53
  95.2 3.4 %fusion.3 = f32[256,64]{0,1:T(8,128)S(1)} fusion(bf16[256,7168]{1,0:T(8,128)(2,1)} %all-gather.2.cloned.1.call-done, bf16[1,64,7168]{2,1,0:T(8,128)(2,1)S(1)} %copy-done), kind=kOutput, calls=%fused_computation.8 | convolution fusion | flops 234881024 | bytes 4653056 | tf_op jit(solution)/shard_map/dot_general | solution.py:23
  98.7 1.2 fusion
  99.9 10.0 %all_to_all.32 = bf16[8,256,64]{1,2,0:T(8,128)(2,1)S(1)} all-to-all(bf16[8,256,64]{1,2,0:T(8,128)(2,1)S(1)} %broadcast_in_dim.20), channel_id=1, replica_groups=mesh['expert'=64,'tensor'=8] {'tensor'}, dimensions={0} | all-to-all | bytes 524288 | tf_op jit(solution)/shard_map/all_to_all | solution.py:15
  109.9 3.0 %convolution_convert_fusion = bf16[8,256,896]{2,1,0:T(8,128)(2,1)} fusion(bf16[64,8,896]{2,0,1:T(8,128)(2,1)S(1)} %all-to-all-done.2, bf16[8,256,64]{1,2,0:T(8,128)(2,1)S(1)} %all_to_all.32), kind=kOutput, calls=%fused_computation.2 | convolution fusion | flops 236716032 | bytes 4849664 | tf_op jit(solution)/shard_map/rgf,gfd->grd/dot_general | solution.py:64
  112.9 2.8 %reduce_sum.31 = bf16[256,896]{1,0:T(8,128)(2,1)S(1)} reduce(bf16[8,256,896]{2,1,0:T(8,128)(2,1)} %convolution_convert_fusion, bf16[]{:T(256)} %constant.31.clone.1), dimensions={0}, to_apply=%region_3.4 | reduce | flops 1605632 | bytes 4128770 | tf_op jit(solution)/shard_map/reduce_sum | solution.py:68
  115.6 0.9 reshape.41
  116.5 10.0 %all-to-all-start.3 = ((bf16[64,4,896]{2,1,0:T(4,128)(2,1)}), bf16[64,4,896]{2,1,0:T(4,128)(2,1)S(1)}, u32[]{:S(2)}, u32[]{:S(2)}) async-start(bf16[64,4,896]{2,1,0:T(4,128)(2,1)} %reshape.41), calls=%async_computation.3 | async-start | bytes 917504 | tf_op jit(solution)/shard_map/all_to_all | solution.py:69
  126.6 0.1 copy.26
  126.6 0.1 reshape.45
  126.7 0.1 copy.20
  126.8 28.0 %all-to-all-done.3 = bf16[64,4,896]{2,1,0:T(4,128)(2,1)S(1)} async-done(((bf16[64,4,896]{2,1,0:T(4,128)(2,1)}), bf16[64,4,896]{2,1,0:T(4,128)(2,1)S(1)}, u32[]{:S(2)}, u32[]{:S(2)}) %all-to-all-start.3) | async-done | bytes 458784 | tf_op jit(solution)/shard_map/all_to_all | solution.py:69
  154.9 0.1 slice_add_fusion
  155.0 0.2 add.33
  155.2 0.8 gather_fusion
  156.0 0.8 fusion.5
  (25 shorter events, 0.3 us)
Async XLA Ops:
  6.5 88.7 %copy-start = (bf16[1,64,7168]{2,1,0:T(8,128)(2,1)S(1)}, bf16[1,64,7168]{2,1,0:T(8,128)(2,1)}, u32[]{:S(2)}) copy-start(bf16[1,64,7168]{2,1,0:T(8,128)(2,1)} %param.9) | copy-start | bytes 2752516
  6.5 88.7 %all-gather.2.cloned.1.call-start = ((), (), s32[]{:S(2)}) async-start(), calls=%async_computation.4 | async-start | bytes 4128768 | tf_op jit(solution)/shard_map/all_gather | solution.py:53
  8.4 1.5 copy-start.4
  8.4 1.7 %copy-start.5 = (bf16[16,896]{1,0:T(8,128)(2,1)S(1)}, bf16[16,896]{1,0:T(8,128)(2,1)}, u32[]{:S(2)}) copy-start(bf16[16,896]{1,0:T(8,128)(2,1)} %param.6) | copy-start | bytes 86020
  9.7 49.1 %copy-start.2 = (bf16[1,64,7168]{2,1,0:T(8,128)(2,1)S(1)}, bf16[1,64,7168]{2,1,0:T(8,128)(2,1)}, u32[]{:S(2)}) copy-start(bf16[1,64,7168]{2,1,0:T(8,128)(2,1)} %param.11) | copy-start | bytes 2752516
  60.0 38.6 %copy-start.3 = (bf16[1,64,7168]{2,1,0:T(8,128)(2,1)S(1)}, bf16[1,64,7168]{2,1,0:T(8,128)(2,1)}, u32[]{:S(2)}) copy-start(bf16[1,64,7168]{2,1,0:T(8,128)(2,1)} %param.10) | copy-start | bytes 2752516
  60.0 39.9 %all-to-all-start.2 = ((bf16[64,8,896]{2,0,1:T(8,128)(2,1)}), bf16[64,8,896]{2,0,1:T(8,128)(2,1)S(1)}, u32[]{:S(2)}, u32[]{:S(2)}) async-start(bf16[64,8,896]{2,0,1:T(8,128)(2,1)} %copy.25), calls=%async_computation.2 | async-start | bytes 1835008 | tf_op jit(solution)/shard_map/all_to_all | solution.py:57
  95.2 3.4 %copy-start.1 = (bf16[256,7168]{1,0:T(8,128)(2,1)S(1)}, bf16[256,7168]{1,0:T(8,128)(2,1)}, u32[]{:S(2)}) copy-start(bf16[256,7168]{1,0:T(8,128)(2,1)} %all-gather.2.cloned.1.call-done) | copy-start | bytes 11010052
  112.9 13.9 %copy-start.6 = (f32[16,8]{0,1:T(8,128)S(1)}, f32[16,8]{0,1:T(8,128)}, u32[]{:S(2)}) copy-start(f32[16,8]{0,1:T(8,128)} %param.8) | copy-start | bytes 1540
  116.5 38.3 %all-to-all-start.3 = ((bf16[64,4,896]{2,1,0:T(4,128)(2,1)}), bf16[64,4,896]{2,1,0:T(4,128)(2,1)S(1)}, u32[]{:S(2)}, u32[]{:S(2)}) async-start(bf16[64,4,896]{2,1,0:T(4,128)(2,1)} %reshape.41), calls=%async_computation.3 | async-start | bytes 917504 | tf_op jit(solution)/shard_map/all_to_all | solution.py:69
Sparse Core Ops, SparseCore 0:
  58.9 36.2 all-gather.1
where the time goes:
time: 164 us
  waiting for transfers between devices  58.6 us (36%)
  blocking collectives  57.4 us (35%)
  starting transfers between devices  14.6 us (9%)
  between operations  13.6 us (8%)
  matrix products  7.88 us (5%)
  local copies, waits for them, and re-layouts  6.9 us (4%)
  other arithmetic  4.69 us (3%)
    all_to_all x1, blocking collectives, body(): lax.all_to_all(jnp.repeat(packed, 2, axis=0), 'expert', split_axis=0, con...  47.4 us
    all_gather x1, waiting for transfers between devices, body(): shard_piece = lax.all_gather(arrived, 'tensor', axis=1, tiled=True)  30.6 us
    all_to_all x1, waiting for transfers between devices, body(): lax.all_to_all(half_out.reshape(devices_wide, capacity, -1), 'expert', sp...  28 us
    all_to_all x1, starting transfers between devices, body(): lax.all_to_all(half_out.reshape(devices_wide, capacity, -1), 'expert', sp...  10 us
    all_to_all x1, blocking collectives, sent_to_all(): return lax.all_to_all(copies, axis, split_axis=0, concat_axis=0, tiled=True)  9.98 us
    dot_general x2, matrix products, rows_times(): lax.dot_general(rows, weight, (((1,), (1,)), ((), ())), preferred_element...  4.66 us
    all_to_all x1, starting transfers between devices, body(): lax.all_to_all(weight_out, 'tensor', split_axis=1, concat_axis=0, tiled=T...  4.6 us
  transfers between devices with their start and end apart: 3, of which 2 were waited for; matrix products, arithmetic and copies ran while one was open for 4% of the time, Pallas kernels for 0%

commit v1 on v0

--- a/solution.py
+++ b/solution.py
@@ -2,6 +2,11 @@
 import jax.numpy as jnp
 from jax import lax
 from jax.sharding import PartitionSpec as P
+
+
+def swapped_in(shard, mesh_axis, along):
+    sent = jnp.stack([shard] * lax.axis_size(mesh_axis))
+    return jnp.concatenate(lax.all_to_all(sent, mesh_axis, 0, 0), axis=along)
 
 
 def in_order(blocks, dim):
@@ -50,7 +55,7 @@
     arrived = lax.all_to_all(
         jnp.repeat(packed, 2, axis=0), "expert", split_axis=0, concat_axis=0, tiled=True
     ).reshape(arrived_count, -1)
-    shard_piece = lax.all_gather(arrived, "tensor", axis=1, tiled=True)
+    shard_piece = swapped_in(arrived, "tensor", 1)
     gate_act = rows_times(shard_piece, weight_gate)
     up_act = rows_times(shard_piece, weight_up)
     hidden = (jax.nn.silu(gate_act) * up_act).astype(jnp.bfloat16)

time: 164 us -> 175 us (1.067)
  waiting for transfers between devices: 58.6 us -> 79.8 us
  between operations: 13.6 us -> 0.21 us
    all_to_all x0 -> x1, waiting for transfers between devices: none -> 42.9 us  [swapped_in(): return jnp.concatenate(lax.all_to_all(sent, mesh_axis, 0, 0), axis=along)]
    all_gather x1 -> x0, waiting for transfers between devices: 30.6 us -> none  [body(): shard_piece = lax.all_gather(arrived, 'tensor', axis=1, tiled=True)]
    all_to_all x1, waiting for transfers between devices: 0.01 us -> 8.92 us  [body(): lax.all_to_all(weight_out, 'tensor', split_axis=1, concat_axis=0, tiled=T...]
    all_to_all x0 -> x1, starting transfers between devices: none -> 4.63 us  [swapped_in(): return jnp.concatenate(lax.all_to_all(sent, mesh_axis, 0, 0), axis=along)]
    all_to_all x1, starting transfers between devices: 10 us -> 6.97 us  [body(): lax.all_to_all(half_out.reshape(devices_wide, capacity, -1), 'expert', sp...]
    another operation x0 -> x3, local copies, waits for them, and re-layouts: none -> 2.39 us  [swapped_in(): sent = jnp.stack([shard] * lax.axis_size(mesh_axis))]
  transfers between devices with their start and end apart: 3 -> 3, of which waited for: 2 -> 3; matrix products, arithmetic and copies ran while one was open for 4% -> 4% of each run, Pallas kernels for 0% -> 0%
where the time goes in v1:
time: 175 us; the launch traced here: 174 us
  waiting for transfers between devices  79.8 us (46%)
  blocking collectives  57.3 us (33%)
  starting transfers between devices  15.2 us (9%)
  matrix products  8.73 us (5%)
  local copies, waits for them, and re-layouts  8.4 us (5%)
  other arithmetic  4.69 us (3%)
    all_to_all x1, blocking collectives, body(): lax.all_to_all(jnp.repeat(packed, 2, axis=0), 'expert', split_axis=0, con...  47.4 us
    all_to_all x1, waiting for transfers between devices, swapped_in(): return jnp.concatenate(lax.all_to_all(sent, mesh_axis, 0, 0), axis=along)  42.9 us
    all_to_all x1, waiting for transfers between devices, body(): lax.all_to_all(half_out.reshape(devices_wide, capacity, -1), 'expert', sp...  28 us
    all_to_all x1, blocking collectives, sent_to_all(): return lax.all_to_all(copies, axis, split_axis=0, concat_axis=0, tiled=True)  9.91 us
    all_to_all x1, waiting for transfers between devices, body(): lax.all_to_all(weight_out, 'tensor', split_axis=1, concat_axis=0, tiled=T...  8.92 us
    all_to_all x1, starting transfers between devices, body(): lax.all_to_all(half_out.reshape(devices_wide, capacity, -1), 'expert', sp...  6.97 us
    dot_general x2, matrix products, rows_times(): lax.dot_general(rows, weight, (((1,), (1,)), ((), ())), preferred_element...  5.5 us
    all_to_all x1, starting transfers between devices, swapped_in(): return jnp.concatenate(lax.all_to_all(sent, mesh_axis, 0, 0), axis=along)  4.63 us
  transfers between devices with their start and end apart: 3, of which 3 were waited for; matrix products, arithmetic and copies ran while one was open for 4% of the time, Pallas kernels for 0%

profile of v1, /device:TPU:6, one launch (start us, length us, event | category | flops | bytes accessed | tf_op | source)
XLA Modules:
  0.0 174.3 jit_solution(16874876397680388563)
XLA Ops:
  0.0 0.8 copy.30
  0.8 0.7 bitcast_or_fusion
  1.5 0.1 convert_reduce_fusion
  1.8 0.1 reshape.57
  1.9 1.3 gather_fusion.1
  3.1 0.1 reshape.60
  3.4 0.1 fusion.7
  3.5 0.3 convolution_convert_fusion.1
  3.9 0.1 broadcast_in_dim.19
  4.0 47.4 %all_to_all.36 = bf16[64,4,896]{2,1,0:T(4,128)(2,1)S(1)} all-to-all(bf16[64,4,896]{2,1,0:T(4,128)(2,1)S(1)} %bitcast.34), channel_id=1, replica_groups=mesh['expert'=64,'tensor'=8] {'expert'}, dimensions={0} | all-to-all | bytes 917504 | tf_op jit(solution)/shard_map/all_to_all | solution.py:55
  51.4 0.1 stack_reshape.2
  51.5 0.2 copy.34
  51.7 2.1 %stack.3 = bf16[8,256,896]{1,2,0:T(8,128)(2,1)} broadcast(bf16[256,896]{0,1:T(8,128)(2,1)S(1)} %copy.34), dimensions={1,2} | broadcast | bytes 4128768 | tf_op jit(solution)/shard_map/stack | solution.py:8
  53.8 4.6 %all-to-all-start.1 = ((bf16[8,256,896]{1,2,0:T(8,128)(2,1)}), bf16[8,256,896]{1,2,0:T(8,128)(2,1)}, u32[]{:S(2)}, u32[]{:S(2)}) async-start(bf16[8,256,896]{1,2,0:T(8,128)(2,1)} %stack.3), calls=%async_computation.1 | async-start | bytes 7340032 | tf_op jit(solution)/shard_map/all_to_all | solution.py:9
  58.4 0.1 copy.37
  58.6 1.1 copy.35
  59.6 42.9 %all-to-all-done.1 = bf16[8,256,896]{1,2,0:T(8,128)(2,1)} async-done(((bf16[8,256,896]{1,2,0:T(8,128)(2,1)}), bf16[8,256,896]{1,2,0:T(8,128)(2,1)}, u32[]{:S(2)}, u32[]{:S(2)}) %all-to-all-start.1) | async-done | bytes 3670048 | tf_op jit(solution)/shard_map/all_to_all | solution.py:9
  102.5 3.6 %all-to-all-start.3 = ((bf16[64,8,896]{2,0,1:T(8,128)(2,1)}), bf16[64,8,896]{2,0,1:T(8,128)(2,1)S(1)}, u32[]{:S(2)}, u32[]{:S(2)}) async-start(bf16[64,8,896]{2,0,1:T(8,128)(2,1)} %copy.35), calls=%async_computation.3 | async-start | bytes 1835008 | tf_op jit(solution)/shard_map/all_to_all | solution.py:62
  106.1 2.7 %fusion.3 = f32[256,64]{0,1:T(8,128)S(1)} fusion(bf16[256,7168]{0,1:T(8,128)(2,1)} %bitcast.3, bf16[1,64,7168]{2,1,0:T(8,128)(2,1)S(1)} %copy-done), kind=kOutput, calls=%fused_computation.8 | convolution fusion | flops 234881024 | bytes 4653056 | tf_op jit(solution)/shard_map/dot_general | solution.py:28
  108.8 2.8 %fusion = bf16[256,64]{0,1:T(8,128)(2,1)S(1)} fusion(bf16[256,7168]{0,1:T(8,128)(2,1)} %bitcast.3, bf16[1,64,7168]{2,1,0:T(8,128)(2,1)S(1)} %copy-done.2, f32[256,64]{0,1:T(8,128)S(1)} %fusion.3), kind=kOutput, calls=%fused_computation.5 | convolution fusion | flops 234979328 | bytes 4685824 | tf_op jit(solution)/shard_map/dot_general | solution.py:28
  111.6 8.9 %all-to-all-done.3 = bf16[64,8,896]{2,0,1:T(8,128)(2,1)S(1)} async-done(((bf16[64,8,896]{2,0,1:T(8,128)(2,1)}), bf16[64,8,896]{2,0,1:T(8,128)(2,1)S(1)}, u32[]{:S(2)}, u32[]{:S(2)}) %all-to-all-start.3) | async-done | bytes 917536 | tf_op jit(solution)/shard_map/all_to_all | solution.py:62
  120.5 9.9 %all_to_all.37 = bf16[8,256,64]{1,2,0:T(8,128)(2,1)S(1)} all-to-all(bf16[8,256,64]{1,2,0:T(8,128)(2,1)S(1)} %broadcast_in_dim.20), channel_id=1, replica_groups=mesh['expert'=64,'tensor'=8] {'tensor'}, dimensions={0} | all-to-all | bytes 524288 | tf_op jit(solution)/shard_map/all_to_all | solution.py:20
  130.4 3.0 %convolution_convert_fusion = bf16[8,256,896]{2,1,0:T(8,128)(2,1)} fusion(bf16[64,8,896]{2,0,1:T(8,128)(2,1)S(1)} %all-to-all-done.3, bf16[8,256,64]{1,2,0:T(8,128)(2,1)S(1)} %all_to_all.37), kind=kOutput, calls=%fused_computation.2 | convolution fusion | flops 236716032 | bytes 4849664 | tf_op jit(solution)/shard_map/rgf,gfd->grd/dot_general | solution.py:69
  133.4 2.8 %reduce_sum.31 = bf16[256,896]{1,0:T(8,128)(2,1)S(1)} reduce(bf16[8,256,896]{2,1,0:T(8,128)(2,1)} %convolution_convert_fusion, bf16[]{:T(256)} %constant.31.clone.1), dimensions={0}, to_apply=%region_3.4 | reduce | flops 1605632 | bytes 4128770 | tf_op jit(solution)/shard_map/reduce_sum | solution.py:73
  136.2 0.9 reshape.47
  137.0 7.0 %all-to-all-start.4 = ((bf16[64,4,896]{2,1,0:T(4,128)(2,1)}), bf16[64,4,896]{2,1,0:T(4,128)(2,1)S(1)}, u32[]{:S(2)}, u32[]{:S(2)}) async-start(bf16[64,4,896]{2,1,0:T(4,128)(2,1)} %reshape.47), calls=%async_computation.4 | async-start | bytes 917504 | tf_op jit(solution)/shard_map/all_to_all | solution.py:74
  144.1 0.1 reshape.51
  144.3 28.0 %all-to-all-done.4 = bf16[64,4,896]{2,1,0:T(4,128)(2,1)S(1)} async-done(((bf16[64,4,896]{2,1,0:T(4,128)(2,1)}), bf16[64,4,896]{2,1,0:T(4,128)(2,1)S(1)}, u32[]{:S(2)}, u32[]{:S(2)}) %all-to-all-start.4) | async-done | bytes 458784 | tf_op jit(solution)/shard_map/all_to_all | solution.py:74
  172.3 0.1 slice_add_fusion
  172.5 0.2 add.33
  172.6 0.8 gather_fusion
  173.5 0.8 fusion.5
  (24 shorter events, 0.6 us)
Async XLA Ops:
  0.0 106.1 %copy-start = (bf16[1,64,7168]{2,1,0:T(8,128)(2,1)S(1)}, bf16[1,64,7168]{2,1,0:T(8,128)(2,1)}, u32[]{:S(2)}) copy-start(bf16[1,64,7168]{2,1,0:T(8,128)(2,1)} %param.9) | copy-start | bytes 2752516
  1.8 1.5 copy-start.3
  1.9 1.6 copy-start.4
  53.8 4.6 %copy-start.1 = (bf16[1,64,7168]{2,1,0:T(8,128)(2,1)S(1)}, bf16[1,64,7168]{2,1,0:T(8,128)(2,1)}, u32[]{:S(2)}) copy-start(bf16[1,64,7168]{2,1,0:T(8,128)(2,1)} %param.11) | copy-start | bytes 2752516
  53.8 48.7 %all-to-all-start.1 = ((bf16[8,256,896]{1,2,0:T(8,128)(2,1)}), bf16[8,256,896]{1,2,0:T(8,128)(2,1)}, u32[]{:S(2)}, u32[]{:S(2)}) async-start(bf16[8,256,896]{1,2,0:T(8,128)(2,1)} %stack.3), calls=%async_computation.1 | async-start | bytes 7340032 | tf_op jit(solution)/shard_map/all_to_all | solution.py:9
  59.6 49.2 %copy-start.2 = (bf16[1,64,7168]{2,1,0:T(8,128)(2,1)S(1)}, bf16[1,64,7168]{2,1,0:T(8,128)(2,1)}, u32[]{:S(2)}) copy-start(bf16[1,64,7168]{2,1,0:T(8,128)(2,1)} %param.10) | copy-start | bytes 2752516
  102.5 18.0 %all-to-all-start.3 = ((bf16[64,8,896]{2,0,1:T(8,128)(2,1)}), bf16[64,8,896]{2,0,1:T(8,128)(2,1)S(1)}, u32[]{:S(2)}, u32[]{:S(2)}) async-start(bf16[64,8,896]{2,0,1:T(8,128)(2,1)} %copy.35), calls=%async_computation.3 | async-start | bytes 1835008 | tf_op jit(solution)/shard_map/all_to_all | solution.py:62
  133.4 10.8 %copy-start.5 = (f32[16,8]{0,1:T(8,128)S(1)}, f32[16,8]{0,1:T(8,128)}, u32[]{:S(2)}) copy-start(f32[16,8]{0,1:T(8,128)} %param.8) | copy-start | bytes 1540
  137.0 35.2 %all-to-all-start.4 = ((bf16[64,4,896]{2,1,0:T(4,128)(2,1)}), bf16[64,4,896]{2,1,0:T(4,128)(2,1)S(1)}, u32[]{:S(2)}, u32[]{:S(2)}) async-start(bf16[64,4,896]{2,1,0:T(4,128)(2,1)} %reshape.47), calls=%async_computation.4 | async-start | bytes 917504 | tf_op jit(solution)/shard_map/all_to_all | solution.py:74
